TPU v7x, 32 devices: a whole 2x2x4 slice. The times are simulated.
32 devices in a mesh: exp: 8 (over z, x), seq: 4 (over y, core).
Axes of the slice: x: 2, y: 2, z: 4, core: 2. Of those that a mesh axis runs over, the one named last changes fastest.
Arguments:
- out_grad: bfloat16 [4096, 4096], P(('exp', 'seq')), may hold values from -1.5 to 1.5
- chosen: int32 [8, 1024], P('exp'), may hold values from 0 to 4095, as said below
- scores: float32 [8, 1024], P('exp'), may hold values from 0.05 to 1
- saved_pre: bfloat16 [8, 1024, 2, 1536], P('exp', None, None, 'seq'), may hold values from -6 to 6
- gate_up: bfloat16 [8, 4096, 2, 1536], P('exp', None, None, 'seq'), may hold values from -0.09375 to 0.09375
- down: bfloat16 [8, 1536, 4096], P('exp', 'seq'), may hold values from -0.15625 to 0.15625
Outputs:
- in_grad: bfloat16 [4096, 4096], P(('exp', 'seq'))
- score_grad: float32 [8, 1024], P('exp')
Inputs may be any that keep to these rules, and one draw needn't show every extreme that they name: `chosen`: each row lists 1024 different tokens. At most 144 of one row's tokens lie in one block of 512 consecutive tokens (the tokens of one index of exp), and every row has exactly 144 in some block.
All inputs are finite; a program needn't handle non-finite values.
Results may differ from a plain program's by a relative error of at most 0.012.
Values may be sent and summed in bfloat16 or wider, within the bound.
A program may use at most 128 MiB of HBM per device.

v0:
```python
import jax
import jax.numpy as jnp
from jax import lax
from jax.sharding import PartitionSpec as P


def local(out_grad, chosen, scores, saved_pre, gate_up, down):
    n_exp = lax.axis_size("exp")
    n_seq = lax.axis_size("seq")
    capacity = chosen.shape[1]
    slot_most = 9 * capacity // (8 * n_exp)
    tok_count = out_grad.shape[0]
    model_width = out_grad.shape[1]
    group_tok = tok_count * n_seq
    pad_rows = n_exp * slot_most
    hidden_part = gate_up.shape[3]
    group_index = lax.axis_index("exp")
    all_ids = lax.all_gather(chosen, "exp", axis=0, tiled=True)
    group_grad = lax.all_gather(out_grad, "seq", axis=0, tiled=True)
    local_ids = all_ids - group_index * group_tok
    inside = (local_ids >= 0) & (local_ids < group_tok)
    slot_rank = jnp.cumsum(inside.astype(jnp.int32), axis=1) - 1
    slot_ids = jnp.arange(slot_most, dtype=jnp.int32)
    picked = inside[:, None, :] & (slot_rank[:, None, :] == slot_ids[None, :, None])
    filled = jnp.any(picked, axis=2).reshape(pad_rows)
    source_row = jnp.sum(jnp.where(picked, local_ids[:, None, :], 0), axis=2).reshape(pad_rows)
    outgoing = jnp.where(filled[:, None], group_grad[source_row], jnp.zeros((), jnp.bfloat16))
    fetched = lax.all_to_all(outgoing, "exp", split_axis=0, concat_axis=0, tiled=True)
    own_ids = chosen[0]
    owner_group = own_ids // group_tok
    owner_hits = (owner_group[:, None] == jnp.arange(n_exp, dtype=jnp.int32)[None, :]).astype(
        jnp.int32
    )
    slot_order = jnp.sum(jnp.cumsum(owner_hits, axis=0) * owner_hits, axis=1) - 1
    position = owner_group * slot_most + slot_order
    down_rows = down[0]
    mixing = gate_up[0].reshape(model_width, 2 * hidden_part)
    pre_padded = jnp.zeros((pad_rows, 2, hidden_part), jnp.bfloat16).at[position].set(saved_pre[0])
    weight_padded = jnp.zeros((pad_rows,), jnp.float32).at[position].set(scores[0])
    back_grad = lax.dot_general(
        fetched, down_rows, (((1,), (1,)), ((), ())), preferred_element_type=jnp.float32
    )
    gate_pre = pre_padded[:, 0].astype(jnp.float32)
    up_pre = pre_padded[:, 1].astype(jnp.float32)
    sigmoid_gate = jax.nn.sigmoid(gate_pre)
    activated = gate_pre * sigmoid_gate
    hidden = (activated * up_pre).astype(jnp.bfloat16)
    hidden = lax.optimization_barrier(hidden)
    score_part = jnp.sum(hidden.astype(jnp.float32) * back_grad, axis=1)
    scaled = weight_padded[:, None] * back_grad
    d_gate = scaled * up_pre * sigmoid_gate * (1.0 + gate_pre * (1.0 - sigmoid_gate))
    d_up = scaled * activated
    d_both = (
        jnp.stack([d_gate, d_up], axis=1)
        .astype(jnp.bfloat16)
        .reshape(fetched.shape[0], 2 * hidden_part)
    )
    partial_value = lax.dot_general(
        d_both, mixing, (((1,), (1,)), ((), ())), preferred_element_type=jnp.float32
    ).astype(jnp.bfloat16)
    partial_value, score_padded = (partial_value, score_part)
    score_part = score_padded[position]
    score_grad = lax.psum(score_part, "seq")[None, :]
    arrived = lax.all_to_all(partial_value, "exp", split_axis=0, concat_axis=0, tiled=True)
    totals = (
        jnp.zeros((group_tok, model_width), jnp.float32)
        .at[source_row]
        .add(arrived.astype(jnp.float32))
    )
    summed = lax.psum_scatter(totals.astype(jnp.bfloat16), "seq", scatter_dimension=0, tiled=True)
    return (summed, score_grad)


def solution(mesh):
    return jax.shard_map(
        local,
        mesh=mesh,
        in_specs=(
            P(("exp", "seq"), None),
            P("exp", None),
            P("exp", None),
            P("exp", None, None, "seq"),
            P("exp", None, None, "seq"),
            P("exp", "seq", None),
        ),
        out_specs=(P(("exp", "seq"), None), P("exp", None)),
        check_vma=False,
    )
```

profile of v0, /device:TPU:0, one launch (start us, length us, event | category | flops | bytes accessed | tf_op | source)
XLA Modules:
  0.0 611.6 jit_solution(15147982498281689753)
XLA Ops:
  7.2 0.7 all-gather.3.cloned.1.call-update
  7.9 32.5 %all-gather = s32[8,1,1024]{2,1,0:T(1,128)S(1)} all-gather(s32[1,1,1024]{2,1,0:T(1,128)} %bitcast.99), channel_id=1, replica_groups=mesh['exp'=8,'seq'=4] {'exp'}, dimensions={0}, use_global_device_ids=true | all-gather | bytes 36864 | tf_op jit(solution)/shard_map/all_gather | solution.py:18
  40.4 2.3 reduce-window.14
  42.7 0.3 slice_reduce_fusion.1
  43.0 0.2 reduce-window.15
  43.3 1.1 select_reduce_fusion
  44.5 0.8 fusion.3
  45.3 1.5 all-gather.3.cloned.1.call-done
  46.8 21.1 %gather_fusion = bf16[1152,4096]{1,0:T(8,128)(2,1)} fusion(bf16[512,4096]{1,0:T(8,128)(2,1)} %all-gather.3.cloned.1.call-done, s32[2048]{0:T(1024)S(1)} %pad_clamp_fusion), kind=kCustom, calls=%fused_computation | custom fusion | bytes 18878976 | tf_op jit(solution)/shard_map/gather | solution.py:27
  67.9 8.0 %broadcast_select_fusion = bf16[8,144,4096]{2,1,0:T(8,128)(2,1)} fusion(bf16[8,144,4096]{2,1,0:T(8,128)(2,1)} %bitcast.87, pred[8,144]{1,0:T(8,128)(4,1)S(1)} %fusion.3), kind=kLoop, calls=%fused_computation.8 | loop fusion | flops 4718592 | bytes 18875520 | tf_op jit(solution)/shard_map/jit(_where)/select_n | solution.py:27
  75.9 5.6 all-to-all-start
  81.6 0.2 reduce-scatter.2.cloned.1.call-start
  81.8 2.3 reduce-window.16
  84.1 0.3 slice_reduce_fusion
  84.7 2.3 broadcast_in_dim.54
  87.0 110.2 %scatter_fusion = bf16[1152,2,384]{2,1,0:T(2,128)(2,1)} fusion(bf16[1152,2,384]{2,1,0:T(2,128)(2,1)} %broadcast_in_dim.54, s32[1024]{0:T(1024)S(1)} %bitcast.102, bf16[1024,2,384]{2,1,0:T(2,128)(2,1)} %bitcast.92), kind=kCustom, calls=%fused_computation.3 | custom fusion | bytes 4722688 | tf_op jit(solution)/shard_map/scatter | solution.py:38
  197.2 6.5 %fusion.27 = (bf16[1152,1,384]{2,1,0:T(2,128)(2,1)}, bf16[1152,1,384]{2,1,0:T(2,128)(2,1)}) fusion(bf16[1152,2,384]{2,1,0:T(2,128)(2,1)} %scatter_fusion), kind=kLoop, calls=%fused_computation.76 | loop fusion | bytes 3538944 | tf_op jit(solution)/shard_map/slice | solution.py:44
  203.6 4.9 copy.18
  208.5 4.8 copy.19
  213.3 2.9 fusion.10
  216.2 6.5 %copy.22 = bf16[512,8,2,384]{3,1,2,0:T(8,128)(2,1)} copy(bf16[512,8,2,384]{3,2,1,0:T(2,128)(2,1)} %bitcast.89) | data formatting | bytes 12582912
  222.7 4.5 scatter_custom_fusion
  227.1 60.5 %all-to-all-done = bf16[8,144,4096]{2,1,0:T(8,128)(2,1)} async-done(((bf16[8,144,4096]{2,1,0:T(8,128)(2,1)}), bf16[8,144,4096]{2,1,0:T(8,128)(2,1)}, u32[]{:S(2)}, u32[]{:S(2)}) %all-to-all-start) | async-done | bytes 9437216 | tf_op jit(solution)/shard_map/all_to_all | solution.py:28
  287.6 11.3 %fusion.16 = (bf16[1152,1,384]{0,2,1:T(8,128)(2,1)S(1)}, bf16[1152,1,384]{0,2,1:T(8,128)(2,1)S(1)}, f32[1152]{0:T(1024)S(1)}) fusion(bf16[1152,1,384]{0,2,1:T(8,128)(2,1)} %copy.19, bf16[1152,1,384]{0,2,1:T(8,128)(2,1)} %copy.18, f32[1152]{0:T(1024)S(1)} %scatter_custom_fusion, bf16[1152,384]{0,1:T(8,128)(2,1)} %fusion.10, bf16[1152,4096]{1,0:T(8,128)(2,1)} %bitcast.10, ...), kind=kOutput, calls=%fused_computation.33 | convolution fusion | flops 3632282624 | bytes 17015808 | tf_op jit(solution)/shard_map/dot_general | solution.py:40
  299.0 0.2 pad_maximum_fusion
  299.2 8.2 %convolution_convert_fusion = bf16[1152,4096]{1,0:T(8,128)(2,1)S(1)} fusion(bf16[1152,768]{0,1:T(8,128)(2,1)S(1)} %bitcast.91, bf16[4096,768]{1,0:T(8,128)(2,1)S(1)} %bitcast.90), kind=kOutput, calls=%fused_computation.7 | convolution fusion | flops 7252475904 | bytes 17498112 | tf_op jit(solution)/shard_map/dot_general | solution.py:58
  307.3 209.2 %all_to_all.18 = bf16[8,144,4096]{2,1,0:T(8,128)(2,1)} all-to-all(bf16[8,144,4096]{2,1,0:T(8,128)(2,1)S(1)} %bitcast.88), channel_id=1, replica_groups=mesh['exp'=8,'seq'=4] {'exp'}, dimensions={0} | all-to-all | bytes 18874368 | tf_op jit(solution)/shard_map/all_to_all | solution.py:64
  516.5 39.5 %scatter_custom_fusion.2 = f32[512,4096]{1,0:T(8,128)} fusion(s32[1152]{0:T(1024)S(1)} %fusion.20, bf16[1152,4096]{1,0:T(8,128)(2,1)} %bitcast.86, f32[]{:T(128)} %constant.17.clone.1), kind=kCustom, calls=%fused_computation.5 | custom fusion | flops 9437184 | bytes 17825796 | tf_op jit(solution)/shard_map/scatter-add | solution.py:68
  556.0 5.9 convert_element_type.56
  562.0 6.2 %gather_fusion.1 = f32[1024]{0:T(1024)S(1)} fusion(f32[1152]{0:T(1024)S(1)} %get-tuple-element.6, s32[1024]{0:T(1024)S(1)} %broadcast_clamp_fusion), kind=kCustom, calls=%fused_computation.1 | custom fusion | bytes 12288 | tf_op jit(solution)/shard_map/gather | solution.py:62
  568.1 6.5 %psum.7 = f32[1,1024]{1,0:T(1,128)} all-reduce(f32[1,1024]{1,0:T(1,128)S(1)} %bitcast.108), channel_id=1, replica_groups=mesh['exp'=8,'seq'=4] {'seq'}, use_global_device_ids=true, to_apply=%region_12.13 | all-reduce | flops 1024 | bytes 8192 | tf_op jit(solution)/shard_map/psum | solution.py:63
  574.7 30.1 %reduce-scatter.2.cloned.1.call-done = bf16[128,4096]{1,0:T(8,128)(2,1)} async-done(((bf16[512,4096]{1,0:T(8,128)(2,1)}), bf16[128,4096]{1,0:T(8,128)(2,1)}) %reduce-scatter.2.cloned.1.call-update) | async-done | bytes 1048592 | tf_op jit(solution)/shard_map/reduce_scatter | solution.py:70
  (28 shorter events, 0.7 us)
Async XLA Ops:
  7.2 280.5 %copy-start = (bf16[1,384,4096]{2,1,0:T(8,128)(2,1)S(1)}, bf16[1,384,4096]{2,1,0:T(8,128)(2,1)}, u32[]{:S(2)}) copy-start(bf16[1,384,4096]{2,1,0:T(8,128)(2,1)} %param.11) | copy-start | bytes 9437188
  7.2 39.6 %all-gather.3.cloned.1.call-start = ((), (), s32[]{:S(2)}) async-start(), calls=%async_computation.3 | async-start | bytes 5242880 | tf_op jit(solution)/shard_map/all_gather | solution.py:19
  75.9 5.9 copy-start.3
  75.9 211.7 %all-to-all-start = ((bf16[8,144,4096]{2,1,0:T(8,128)(2,1)}), bf16[8,144,4096]{2,1,0:T(8,128)(2,1)}, u32[]{:S(2)}, u32[]{:S(2)}) async-start(bf16[8,144,4096]{2,1,0:T(8,128)(2,1)} %broadcast_select_fusion), calls=%async_computation | async-start | bytes 18874368 | tf_op jit(solution)/shard_map/all_to_all | solution.py:28
  81.6 523.2 %reduce-scatter.2.cloned.1.call-start = ((), (), s32[]{:S(2)}) async-start(), calls=%async_computation.4 | async-start | bytes 5242880 | tf_op jit(solution)/shard_map/reduce_scatter | solution.py:70
  287.6 11.5 %copy-start.2 = (bf16[512,8,2,384]{3,1,2,0:T(8,128)(2,1)S(1)}, bf16[512,8,2,384]{3,1,2,0:T(8,128)(2,1)}, u32[]{:S(2)}) copy-start(bf16[512,8,2,384]{3,1,2,0:T(8,128)(2,1)} %copy.22) | copy-start | bytes 18874372
  562.0 42.8 %copy-start.1 = (bf16[1,384,4096]{2,1,0:T(8,128)(2,1)S(1)}, bf16[1,384,4096]{2,1,0:T(8,128)(2,1)}, u32[]{:S(2)}) copy-start(bf16[1,384,4096]{2,1,0:T(8,128)(2,1)} %param.11) | copy-start | bytes 9437188
Sparse Core Ops, SparseCore 0:
  9.6 37.1 all-gather.2
  562.1 42.6 reduce-scatter.1
where the time goes:
time: 617 us; the launch traced here: 612 us
  blocking collectives  248 us (40%)
  local copies, waits for them, and re-layouts  168 us (27%)
  waiting for transfers between devices  92.8 us (15%)
  other arithmetic  63.5 us (10%)
  matrix products  19.5 us (3%)
  between operations  14.2 us (2%)
    all_to_all x1, blocking collectives, local(): lax.all_to_all(partial_value, 'exp', split_axis=0, concat_axis=0, tiled=T...  209 us
    scatter x1, local copies, waits for them, and re-layouts, local(): jnp.zeros((pad_rows, 2, hidden_part), jnp.bfloat16).at[position]  110 us
    all_to_all x1, waiting for transfers between devices, local(): lax.all_to_all(outgoing, 'exp', split_axis=0, concat_axis=0, tiled=True)  60.5 us
    scatter-add x1, other arithmetic, local(): totals = jnp.zeros((group_tok, model_width), jnp.float32).at[source_row]....  39.5 us
    all_gather x1, blocking collectives, local(): all_ids = lax.all_gather(chosen, 'exp', axis=0, tiled=True)  32.5 us
    reduce_scatter x1, waiting for transfers between devices, local(): lax.psum_scatter(totals.astype(jnp.bfloat16), 'seq', scatter_dimension=0,...  30.1 us
    gather x1, local copies, waits for them, and re-layouts, local(): group_grad[source_row]  21.1 us
    unnamed x13, local copies, waits for them, and re-layouts  16.2 us
  transfers between devices with their start and end apart: 3, of which 3 were waited for; matrix products, arithmetic and copies ran while one was open for 26% of the time, Pallas kernels for 0%

commit v1 on v0

--- a/solution.py
+++ b/solution.py
@@ -2,6 +2,29 @@
 import jax.numpy as jnp
 from jax import lax
 from jax.sharding import PartitionSpec as P
+
+
+def cut_along(x, dim, size):
+    dims = x.shape
+    parts = x.reshape(*dims[:dim], size, dims[dim] // size, *dims[dim + 1 :])
+    return jnp.moveaxis(parts, dim, 0)
+
+
+def in_order(parts, dim):
+    shape = list(parts.shape[1:])
+    shape[dim] *= parts.shape[0]
+    return jnp.moveaxis(parts, 0, dim).reshape(shape)
+
+
+def pairwise_exchange(shard, axis, split_dim, concat_dim):
+    count, place = (lax.axis_size(axis), lax.axis_index(axis))
+    blocks = cut_along(shard, split_dim, count)
+    finished = [blocks[place]]
+    for lap in range(1, count):
+        sent = blocks[place ^ lap]
+        finished.append(lax.ppermute(sent, axis, [(i, i ^ lap) for i in range(count)]))
+    blocks = jnp.stack(finished)[place ^ jnp.arange(count)]
+    return in_order(blocks, concat_dim)
 
 
 def local(out_grad, chosen, scores, saved_pre, gate_up, down):
@@ -25,7 +48,7 @@
     filled = jnp.any(picked, axis=2).reshape(pad_rows)
     source_row = jnp.sum(jnp.where(picked, local_ids[:, None, :], 0), axis=2).reshape(pad_rows)
     outgoing = jnp.where(filled[:, None], group_grad[source_row], jnp.zeros((), jnp.bfloat16))
-    fetched = lax.all_to_all(outgoing, "exp", split_axis=0, concat_axis=0, tiled=True)
+    fetched = pairwise_exchange(outgoing, "exp", 0, 0)
     own_ids = chosen[0]
     owner_group = own_ids // group_tok
     owner_hits = (owner_group[:, None] == jnp.arange(n_exp, dtype=jnp.int32)[None, :]).astype(

time: 617 us -> 762 us (1.24)
  waiting for transfers between devices: 92.8 us -> 174 us
  blocking collectives: 248 us -> 280 us
  local copies, waits for them, and re-layouts: 168 us -> 190 us
    ppermute x0 -> x7, waiting for transfers between devices: none -> 142 us  [pairwise_exchange(): lax.ppermute(sent, axis, [(i, i ^ lap) for i in range(count)])]
    all_to_all x1 -> x0, waiting for transfers between devices: 60.5 us -> none  [local(): lax.all_to_all(outgoing, 'exp', split_axis=0, concat_axis=0, tiled=True)]
    all_to_all x1, blocking collectives: 209 us -> 241 us  [local(): lax.all_to_all(partial_value, 'exp', split_axis=0, concat_axis=0, tiled=T...]
    ppermute x0 -> x7, starting transfers between devices: none -> 13.2 us  [pairwise_exchange(): lax.ppermute(sent, axis, [(i, i ^ lap) for i in range(count)])]
    gather x0 -> x1, local copies, waits for them, and re-layouts: none -> 8.89 us  [pairwise_exchange(): blocks = jnp.stack(finished)[place ^ jnp.arange(count)]]
    unnamed x13 -> x21, local copies, waits for them, and re-layouts: 16.2 us -> 24.2 us
  transfers between devices with their start and end apart: 3 -> 9, of which waited for: 3 -> 4; matrix products, arithmetic and copies ran while one was open for 26% -> 21% of each run, Pallas kernels for 0% -> 0%
where the time goes in v1:
time: 762 us; the launch traced here: 757 us
  blocking collectives  280 us (37%)
  local copies, waits for them, and re-layouts  190 us (25%)
  waiting for transfers between devices  174 us (23%)
  other arithmetic  63.6 us (8%)
  matrix products  22.2 us (3%)
  between operations  14.3 us (2%)
  starting transfers between devices  13.2 us (2%)
    all_to_all x1, blocking collectives, local(): lax.all_to_all(partial_value, 'exp', split_axis=0, concat_axis=0, tiled=T...  241 us
    ppermute x7, waiting for transfers between devices, pairwise_exchange(): lax.ppermute(sent, axis, [(i, i ^ lap) for i in range(count)])  142 us
    scatter x1, local copies, waits for them, and re-layouts, local(): jnp.zeros((pad_rows, 2, hidden_part), jnp.bfloat16).at[position]  110 us
    scatter-add x1, other arithmetic, local(): totals = jnp.zeros((group_tok, model_width), jnp.float32).at[source_row]....  39.5 us
    all_gather x1, blocking collectives, local(): all_ids = lax.all_gather(chosen, 'exp', axis=0, tiled=True)  32.5 us
    reduce_scatter x1, waiting for transfers between devices, local(): lax.psum_scatter(totals.astype(jnp.bfloat16), 'seq', scatter_dimension=0,...  31.2 us
    unnamed x21, local copies, waits for them, and re-layouts  24.2 us
    gather x1, local copies, waits for them, and re-layouts, local(): group_grad[source_row]  21.2 us
  transfers between devices with their start and end apart: 9, of which 4 were waited for; matrix products, arithmetic and copies ran while one was open for 21% of the time, Pallas kernels for 0%

profile of v1, /device:TPU:0, one launch (start us, length us, event | category | flops | bytes accessed | tf_op | source)
XLA Modules:
  0.0 757.3 jit_solution(6673524989658875625)
XLA Ops:
  8.0 32.5 %all-gather = s32[8,1,1024]{2,1,0:T(1,128)S(1)} all-gather(s32[1,1,1024]{2,1,0:T(1,128)} %bitcast.130), channel_id=1, replica_groups=mesh['exp'=8,'seq'=4] {'exp'}, dimensions={0}, use_global_device_ids=true | all-gather | bytes 36864 | tf_op jit(solution)/shard_map/all_gather | solution.py:41
  40.5 2.3 reduce-window.14
  44.5 2.3 reduce-window.16
  47.4 2.3 broadcast_in_dim.55
  49.7 110.1 %scatter_fusion = bf16[1152,2,384]{2,1,0:T(2,128)(2,1)} fusion(bf16[1152,2,384]{2,1,0:T(2,128)(2,1)} %broadcast_in_dim.55, s32[1024]{0:T(1024)S(1)} %bitcast.133, bf16[1024,2,384]{2,1,0:T(2,128)(2,1)} %bitcast.123), kind=kCustom, calls=%fused_computation.4 | custom fusion | bytes 4722688 | tf_op jit(solution)/shard_map/scatter | solution.py:61
  160.6 21.2 %gather_fusion = bf16[1152,4096]{1,0:T(8,128)(2,1)} fusion(bf16[512,4096]{1,0:T(8,128)(2,1)} %all-gather.3.cloned.1.call-done, s32[2048]{0:T(1024)S(1)} %pad_clamp_fusion), kind=kCustom, calls=%fused_computation | custom fusion | bytes 18878976 | tf_op jit(solution)/shard_map/gather | solution.py:50
  181.8 8.0 %broadcast_select_fusion = bf16[8,144,4096]{2,1,0:T(8,128)(2,1)} fusion(bf16[8,144,4096]{2,1,0:T(8,128)(2,1)} %bitcast.117, pred[8,144]{1,0:T(8,128)(4,1)S(1)} %fusion.3), kind=kLoop, calls=%fused_computation.9 | loop fusion | flops 4718592 | bytes 18875520 | tf_op jit(solution)/shard_map/jit(_where)/select_n | solution.py:50
  189.8 7.5 dynamic-slice_bitcast_fusion
  198.9 3.7 fusion.28
  202.5 4.8 copy.18
  207.3 4.8 copy.19
  212.1 2.9 fusion.10
  215.0 6.5 copy.22
  221.5 4.5 scatter_custom_fusion
  226.1 2.0 collective-permute-start.2
  228.1 2.1 collective-permute-start.3
  230.2 1.8 collective-permute-start.4
  232.0 3.4 collective-permute-start.5
  235.4 2.4 bitcast_dynamic-update-slice_fusion.6
  237.8 58.3 %collective-permute-done.1 = bf16[144,4096]{1,0:T(8,128)(2,1)S(1)} collective-permute-done((bf16[144,4096]{1,0:T(8,128)(2,1)}, bf16[144,4096]{1,0:T(8,128)(2,1)S(1)}, u32[]{:S(2)}, u32[]{:S(2)}) %collective-permute-start.1) | collective-permute-done | bytes 1179680 | tf_op jit(solution)/shard_map/ppermute | solution.py:25
  296.1 2.3 collective-permute-start.6
  299.5 19.5 %collective-permute-done.2 = bf16[144,4096]{1,0:T(8,128)(2,1)S(1)} collective-permute-done((bf16[144,4096]{1,0:T(8,128)(2,1)}, bf16[144,4096]{1,0:T(8,128)(2,1)S(1)}, u32[]{:S(2)}, u32[]{:S(2)}) %collective-permute-start.2) | collective-permute-done | bytes 1179680 | tf_op jit(solution)/shard_map/ppermute | solution.py:25
  321.3 64.2 %collective-permute-done.4 = bf16[144,4096]{1,0:T(8,128)(2,1)S(1)} collective-permute-done((bf16[144,4096]{1,0:T(8,128)(2,1)}, bf16[144,4096]{1,0:T(8,128)(2,1)S(1)}, u32[]{:S(2)}, u32[]{:S(2)}) %collective-permute-start.4) | collective-permute-done | bytes 1179680 | tf_op jit(solution)/shard_map/ppermute | solution.py:25
  388.9 8.9 %gather_fusion.1 = bf16[8,144,4096]{2,1,0:T(8,128)(2,1)} fusion(bf16[8,144,4096]{2,1,0:T(8,128)(2,1)} %bitcast_dynamic-update-slice_fusion, s32[1024]{0:T(1024)S(1)} %pad_clamp_fusion.1), kind=kCustom, calls=%fused_computation.1 | custom fusion | bytes 18874400 | tf_op jit(solution)/shard_map/gather | solution.py:26
  397.8 11.2 %fusion.16 = (bf16[1152,1,384]{0,2,1:T(8,128)(2,1)S(1)}, bf16[1152,1,384]{0,2,1:T(8,128)(2,1)S(1)}, f32[1152]{0:T(1024)S(1)}) fusion(bf16[1152,1,384]{0,2,1:T(8,128)(2,1)} %copy.19, bf16[1152,1,384]{0,2,1:T(8,128)(2,1)} %copy.18, f32[1152]{0:T(1024)S(1)} %scatter_custom_fusion, bf16[1152,384]{0,1:T(8,128)(2,1)} %fusion.10, ...), kind=kOutput, calls=%fused_computation.49 | convolution fusion | flops 3632282624 | bytes 17015808 | tf_op jit(solution)/shard_map/dot_general | solution.py:63
  409.2 11.0 %convolution_convert_fusion = bf16[1152,4096]{1,0:T(8,128)(2,1)S(1)} fusion(bf16[1152,768]{0,1:T(8,128)(2,1)S(1)} %bitcast.122, bf16[4096,768]{1,0:T(8,128)(2,1)} %bitcast.121), kind=kOutput, calls=%fused_computation.8 | convolution fusion | flops 7252475904 | bytes 17498112 | tf_op jit(solution)/shard_map/dot_general | solution.py:81
  420.2 241.2 %all_to_all.9 = bf16[8,144,4096]{2,1,0:T(8,128)(2,1)} all-to-all(bf16[8,144,4096]{2,1,0:T(8,128)(2,1)S(1)} %bitcast.118), channel_id=1, replica_groups=mesh['exp'=8,'seq'=4] {'exp'}, dimensions={0} | all-to-all | bytes 18874368 | tf_op jit(solution)/shard_map/all_to_all | solution.py:87
  661.4 39.5 %scatter_custom_fusion.2 = f32[512,4096]{1,0:T(8,128)} fusion(s32[1152]{0:T(1024)S(1)} %fusion.20, bf16[1152,4096]{1,0:T(8,128)(2,1)} %bitcast.116, f32[]{:T(128)} %constant.21.clone.1), kind=kCustom, calls=%fused_computation.6 | custom fusion | flops 9437184 | bytes 17825796 | tf_op jit(solution)/shard_map/scatter-add | solution.py:91
  700.8 5.9 convert_element_type.56
  706.8 6.2 gather_fusion.2
  713.0 6.3 psum.7
  719.2 31.2 %reduce-scatter.2.cloned.1.call-done = bf16[128,4096]{1,0:T(8,128)(2,1)} async-done(((bf16[512,4096]{1,0:T(8,128)(2,1)}), bf16[128,4096]{1,0:T(8,128)(2,1)}) %reduce-scatter.2.cloned.1.call-update) | async-done | bytes 1048592 | tf_op jit(solution)/shard_map/reduce_scatter | solution.py:93
  (53 shorter events, 12.6 us)
Async XLA Ops:
  7.2 390.7 %copy-start = (bf16[1,384,4096]{2,1,0:T(8,128)(2,1)S(1)}, bf16[1,384,4096]{2,1,0:T(8,128)(2,1)}, u32[]{:S(2)}) copy-start(bf16[1,384,4096]{2,1,0:T(8,128)(2,1)} %param.11) | copy-start | bytes 9437188
  7.2 37.3 %copy-start.4 = (s32[1,1024]{1,0:T(1,128)S(1)}, s32[1,1024]{1,0:T(1,128)}, u32[]{:S(2)}) copy-start(s32[1,1024]{1,0:T(1,128)} %param.7) | copy-start | bytes 12292
  7.2 153.4 %all-gather.3.cloned.1.call-start = ((), (), s32[]{:S(2)}) async-start(), calls=%async_computation.2 | async-start | bytes 5242880 | tf_op jit(solution)/shard_map/all_gather | solution.py:42
  7.9 742.5 %reduce-scatter.2.cloned.1.call-start = ((), (), s32[]{:S(2)}) async-start(), calls=%async_computation.3 | async-start | bytes 5242880 | tf_op jit(solution)/shard_map/reduce_scatter | solution.py:93
  189.8 9.0 %copy-start.2 = (bf16[1152,2,384]{2,1,0:T(2,128)(2,1)S(1)}, bf16[1152,2,384]{2,1,0:T(2,128)(2,1)}, u32[]{:S(2)}) copy-start(bf16[1152,2,384]{2,1,0:T(2,128)(2,1)} %scatter_fusion) | copy-start | bytes 5308420
  197.3 34.7 %collective-permute-start = (bf16[144,4096]{1,0:T(8,128)(2,1)}, bf16[144,4096]{1,0:T(8,128)(2,1)}, u32[]{:S(2)}, u32[]{:S(2)}) collective-permute-start(bf16[144,4096]{1,0:T(8,128)(2,1)} %get-tuple-element.10), channel_id=1, source_target_pairs={{0,4},{4,0},{8,12},{12,8},{16,20},{20,16},{24,28},{28,24},{1,5},{5... | collective-permute-start | bytes 3538952 | tf_op jit(solution)/shard_map/ppermute | solution.py:25
  226.0 70.2 %copy-start.3 = (bf16[144,4096]{1,0:T(8,128)(2,1)S(1)}, bf16[144,4096]{1,0:T(8,128)(2,1)}, u32[]{:S(2)}) copy-start(bf16[144,4096]{1,0:T(8,128)(2,1)} %get-tuple-element.4) | copy-start | bytes 3538948
  226.0 70.1 %collective-permute-start.1 = (bf16[144,4096]{1,0:T(8,128)(2,1)}, bf16[144,4096]{1,0:T(8,128)(2,1)S(1)}, u32[]{:S(2)}, u32[]{:S(2)}) collective-permute-start(bf16[144,4096]{1,0:T(8,128)(2,1)} %get-tuple-element.9), channel_id=1, source_target_pairs={{0,8},{4,12},{8,0},{12,4},{16,24},{20,28},{24,16},{28,20},{1,9},{5... | collective-permute-start | bytes 3538952 | tf_op jit(solution)/shard_map/ppermute | solution.py:25
  226.1 92.9 %collective-permute-start.2 = (bf16[144,4096]{1,0:T(8,128)(2,1)}, bf16[144,4096]{1,0:T(8,128)(2,1)S(1)}, u32[]{:S(2)}, u32[]{:S(2)}) collective-permute-start(bf16[144,4096]{1,0:T(8,128)(2,1)} %get-tuple-element.8), channel_id=1, source_target_pairs={{0,12},{4,8},{8,4},{12,0},{16,28},{20,24},{24,20},{28,16},{1,13},{... | collective-permute-start | bytes 3538952 | tf_op jit(solution)/shard_map/ppermute | solution.py:25
  228.1 92.0 %collective-permute-start.3 = (bf16[144,4096]{1,0:T(8,128)(2,1)}, bf16[144,4096]{1,0:T(8,128)(2,1)S(1)}, u32[]{:S(2)}, u32[]{:S(2)}) collective-permute-start(bf16[144,4096]{1,0:T(8,128)(2,1)} %get-tuple-element.7), channel_id=1, source_target_pairs={{0,16},{4,20},{8,24},{12,28},{16,0},{20,4},{24,8},{28,12},{1,17},{... | collective-permute-start | bytes 3538952 | tf_op jit(solution)/shard_map/ppermute | solution.py:25
  230.2 155.3 %collective-permute-start.4 = (bf16[144,4096]{1,0:T(8,128)(2,1)}, bf16[144,4096]{1,0:T(8,128)(2,1)S(1)}, u32[]{:S(2)}, u32[]{:S(2)}) collective-permute-start(bf16[144,4096]{1,0:T(8,128)(2,1)} %get-tuple-element.6), channel_id=1, source_target_pairs={{0,20},{4,16},{8,28},{12,24},{16,4},{20,0},{24,12},{28,8},{1,21},{... | collective-permute-start | bytes 3538952 | tf_op jit(solution)/shard_map/ppermute | solution.py:25
  232.0 154.6 %collective-permute-start.5 = (bf16[144,4096]{1,0:T(8,128)(2,1)}, bf16[144,4096]{1,0:T(8,128)(2,1)S(1)}, u32[]{:S(2)}, u32[]{:S(2)}) collective-permute-start(bf16[144,4096]{1,0:T(8,128)(2,1)} %get-tuple-element.5), channel_id=1, source_target_pairs={{0,24},{4,28},{8,16},{12,20},{16,8},{20,12},{24,0},{28,4},{1,25},{... | collective-permute-start | bytes 3538952 | tf_op jit(solution)/shard_map/ppermute | solution.py:25
  296.1 91.6 %collective-permute-start.6 = (bf16[144,4096]{1,0:T(8,128)(2,1)S(1)}, bf16[144,4096]{1,0:T(8,128)(2,1)S(1)}, u32[]{:S(2)}, u32[]{:S(2)}) collective-permute-start(bf16[144,4096]{1,0:T(8,128)(2,1)S(1)} %copy-done.3), channel_id=1, source_target_pairs={{0,28},{4,24},{8,20},{12,16},{16,12},{20,8},{24,4},{28,0},{1,29},{... | collective-permute-start | bytes 3538952 | tf_op jit(solution)/shard_map/ppermute | solution.py:25
  706.8 43.7 %copy-start.1 = (bf16[1,384,4096]{2,1,0:T(8,128)(2,1)S(1)}, bf16[1,384,4096]{2,1,0:T(8,128)(2,1)}, u32[]{:S(2)}) copy-start(bf16[1,384,4096]{2,1,0:T(8,128)(2,1)} %param.11) | copy-start | bytes 9437188
Sparse Core Ops, SparseCore 0:
  9.6 37.1 all-gather.2
  706.9 43.5 reduce-scatter.1
